TPU v7x, 512 devices: a whole 4x8x8 slice. The times are simulated.
512 devices in a mesh: ctx: 32 (over y, x), head: 16 (over z, core).
Axes of the slice: x: 4, y: 8, z: 8, core: 2. Of those that a mesh axis runs over, the one named last changes fastest.
Arguments:
- activations: bfloat16 [8192, 16384], P('ctx'), may hold values from -6 to 6
- w_query: bfloat16 [16384, 2048], P('ctx', 'head'), may hold values from -0.046875 to 0.046875
- w_keyval: bfloat16 [16384, 256], P('ctx', 'head'), may hold values from -0.046875 to 0.046875
- f_query: bfloat16 [16, 128, 128], P('head'), may hold values from -1 to 1
- f_key: bfloat16 [128, 128], replicated, may hold values from -1 to 1
- w_out: bfloat16 [2048, 16384], P('ctx', 'head'), may hold values from -0.75 to 0.75
Outputs:
- sublayer_out: bfloat16 [8192, 16384], P('ctx', 'head')
All inputs are finite; a program needn't handle non-finite values.
Results may differ from a plain program's by a relative error of at most 0.0086.
Values may be sent and summed in bfloat16 or wider, within the bound.
A program may use at most 64 MiB of HBM per device.

v0:
```python
import math

import jax
import jax.numpy as jnp
from jax import lax
from jax.sharding import PartitionSpec as P

WINDOW = 64


def from_behind(array, axis, by):
    size = lax.axis_size(axis)
    pairs = [(i, i + by) for i in range(size) if 0 <= i + by < size]
    return lax.ppermute(array, axis, pairs)


def prefix(array, axis, combine, identity):
    size, mine = (lax.axis_size(axis), lax.axis_index(axis))
    everything = jax.tree.map(
        lambda part, kind: lax.all_gather(part.astype(kind), axis),
        array,
        jax.tree.map(lambda a: jnp.bfloat16 if a.dtype == jnp.float32 else a.dtype, array),
    )
    start = jax.tree.map(
        lambda part, zero: jnp.broadcast_to(jnp.asarray(zero, part.dtype), part.shape),
        array,
        identity,
    )

    def step(k, before):
        reached = k < mine
        new = combine(
            before, jax.tree.map(lambda part, own: part[k].astype(own.dtype), everything, array)
        )
        return jax.tree.map(lambda a, b: jnp.where(reached, a, b), new, before)

    return lax.fori_loop(0, size, step, start)


def normalized(logits):
    rising = jnp.exp(logits)
    falling = jnp.exp(-logits)
    rising = rising / jnp.sum(rising, axis=-1, keepdims=True)
    falling = falling / jnp.sum(falling, axis=-1, keepdims=True)
    return jnp.concatenate([rising, falling], axis=-1).astype(jnp.bfloat16)


def state_of(features, values):
    matrix = jnp.einsum("nf,nc->fc", features, values, preferred_element_type=jnp.float32)
    totals = jnp.sum(features.astype(jnp.float32), axis=0)
    return (matrix, totals)


def add_states(earlier, later):
    return (earlier[0] + later[0], earlier[1] + later[1])


def per_device(activations, w_query, w_keyval, f_query, f_key, w_out):
    length = activations.shape[0]
    head_width = f_key.shape[0]
    local_heads = f_query.shape[0]
    columns = activations
    query_sum = jnp.dot(
        columns,
        lax.all_gather(w_query, "ctx", axis=0, tiled=True),
        preferred_element_type=jnp.float32,
    )
    pair_sum = jnp.dot(
        columns,
        lax.all_gather(w_keyval, "ctx", axis=0, tiled=True),
        preferred_element_type=jnp.float32,
    )
    queries = query_sum.astype(jnp.bfloat16)
    keyval = lax.all_gather(pair_sum.astype(jnp.bfloat16), "head", axis=1, tiled=True)
    border = from_behind(keyval[length - WINDOW :], "ctx", 1)
    extended = jnp.concatenate([border, keyval], axis=0)
    ext_keys = extended[:, :head_width]
    ext_vals = extended[:, head_width:]
    first_pos = lax.axis_index("ctx") * length - WINDOW
    present = first_pos + jnp.arange(length + WINDOW) >= 0
    ext_feats = normalized(jnp.dot(ext_keys, f_key, preferred_element_type=jnp.float32))
    ext_feats = jnp.where(present[:, None], ext_feats, jnp.zeros_like(ext_feats))
    contribution = state_of(ext_feats[:length], ext_vals[:length])
    identity = (
        jnp.zeros((2 * head_width, head_width), jnp.float32),
        jnp.zeros((2 * head_width,), jnp.float32),
    )
    matrix, totals = prefix(contribution, "ctx", add_states, identity)
    query_heads = queries.reshape(length, local_heads, head_width)
    query_feats = normalized(
        jnp.einsum("thc,hcf->htf", query_heads, f_query, preferred_element_type=jnp.float32)
    )
    offsets = jnp.arange(length)[:, None] + WINDOW - jnp.arange(length + WINDOW)[None, :]
    inside = (offsets >= 0) & (offsets < WINDOW) & present[None, :]
    beyond = (offsets >= WINDOW) & present[None, :]
    scale = 1.0 / math.sqrt(head_width)
    scores = (
        jnp.einsum("thc,kc->htk", query_heads, ext_keys, preferred_element_type=jnp.float32) * scale
    )
    near_w = jnp.where(inside[None], jnp.exp(scores), 0.0)
    far_w = jnp.where(
        beyond[None],
        jnp.einsum("htf,kf->htk", query_feats, ext_feats, preferred_element_type=jnp.float32),
        0.0,
    )
    weights = near_w + far_w
    feats_wide = query_feats.astype(jnp.float32)
    numerator = jnp.einsum(
        "htk,kc->htc", weights, ext_vals.astype(jnp.float32), precision=lax.Precision.HIGHEST
    )
    numerator = numerator + jnp.einsum(
        "htf,fc->htc", feats_wide, matrix, precision=lax.Precision.HIGHEST
    )
    denominator = jnp.sum(weights, axis=-1) + jnp.einsum(
        "htf,f->ht", feats_wide, totals, precision=lax.Precision.HIGHEST
    )
    attn_heads = (numerator / denominator[..., None]).astype(jnp.bfloat16)
    attn_rows = jnp.transpose(attn_heads, (1, 0, 2)).reshape(length, local_heads * head_width)
    all_heads = lax.all_gather(attn_rows, "head", axis=1, tiled=True)
    columns = all_heads
    projected = jnp.dot(
        columns,
        lax.all_gather(w_out, "ctx", axis=0, tiled=True),
        preferred_element_type=jnp.float32,
    )
    return projected.astype(jnp.bfloat16)


def solution(mesh):
    in_specs = (
        P("ctx", None),
        P("ctx", "head"),
        P("ctx", "head"),
        P("head", None, None),
        P(),
        P("ctx", "head"),
    )
    out_specs = P("ctx", "head")
    return jax.shard_map(
        per_device, mesh=mesh, in_specs=in_specs, out_specs=out_specs, check_vma=False
    )
```

profile of v0, /device:TPU:1, one launch (start us, length us, event | category | flops | bytes accessed | tf_op | source)
XLA Modules:
  0.0 402.4 jit_solution(3140013990136511824)
XLA Ops:
  6.5 39.9 %all_gather.27 = bf16[16384,16]{0,1:T(8,128)(2,1)S(1)} all-gather(bf16[512,16]{0,1:T(8,128)(2,1)} %param.10), channel_id=1, replica_groups=mesh['ctx'=32,'head'=16] {'ctx'}, dimensions={0}, use_global_device_ids=true | all-gather | bytes 540672 | tf_op jit(solution)/shard_map/all_gather | solution.py:70
  46.5 5.6 %convolution_convert_fusion.3 = bf16[256,16]{0,1:T(8,128)(2,1)S(1)} fusion(bf16[256,16384]{1,0:T(8,128)(2,1)} %param.8, bf16[16384,16]{0,1:T(8,128)(2,1)S(1)} %all_gather.27), kind=kOutput, calls=%fused_computation.16 | convolution fusion | flops 134221824 | bytes 8921088 | tf_op jit(solution)/shard_map/dot_general | solution.py:68
  52.1 35.5 %all_gather.28 = bf16[256,256]{0,1:T(8,128)(2,1)S(1)} all-gather(bf16[256,16]{0,1:T(8,128)(2,1)S(1)} %convolution_convert_fusion.3), channel_id=1, replica_groups=mesh['ctx'=32,'head'=16] {'head'}, dimensions={1}, use_global_device_ids=true | all-gather | bytes 139264 | tf_op jit(solution)/shard_map/all_gather | solution.py:74
  87.6 0.1 slice.21
  87.7 2.4 collective-permute-start
  90.1 1.3 collective-permute-done
  91.4 0.5 exponential_reduce_fusion
  91.9 0.2 divide_convert_fusion.1
  92.1 0.1 maximum_select_fusion
  92.2 0.9 convolution_convert_fusion.1
  93.1 0.0 all-gather.14.cloned.1.call-update
  93.1 0.0 all-gather.8.cloned.1.call-start
  93.2 0.7 all-gather.8.cloned.1.call-update
  93.9 0.0 all-gather.12.cloned.1.call-start
  93.9 0.7 all-gather.12.cloned.1.call-update
  94.6 0.0 all-gather.10.cloned.1.call-start
  94.7 0.1 slice_reduce_fusion
  94.7 35.3 %all-gather.2 = bf16[32,1,256]{2,1,0:T(2,128)(2,1)S(1)} all-gather(bf16[1,1,256]{2,1,0:T(2,128)(2,1)S(1)} %reshape.161), channel_id=3, replica_groups=mesh['ctx'=32,'head'=16] {'ctx'}, dimensions={0}, use_global_device_ids=true | all-gather | bytes 16896 | tf_op jit(solution)/shard_map/all_gather | solution.py:20
  130.0 41.1 %all-gather.14.cloned.1.call-done = bf16[8192,128]{1,0:T(8,128)(2,1)} async-done(((bf16[256,128]{1,0:T(8,128)(2,1)}), bf16[8192,128]{1,0:T(8,128)(2,1)}) %all-gather.14.cloned.1.call-update) | async-done | bytes 2097168 | tf_op jit(solution)/shard_map/all_gather | solution.py:20
  171.1 30.8 %while.16 = (s32[]{:T(128)}, f32[256,128]{1,0:T(8,128)S(1)}, f32[256]{0:T(256)S(1)}, s32[]{:T(128)}, bf16[32,256,128]{2,1,0:T(8,128)(2,1)}, /*index=5*/bf16[32,256]{1,0:T(8,128)(2,1)S(1)}, s32[]{:T(128)}, s32[]{:T(128)}) while((s32[]{:T(128)}, f32[256,128]{1,0:T(8,128)S(1)}, f32[256]{0:T(256)S(1)}, s32[]{:T(128)}, ...), condition=%wide.region_6.7_spmd.clone, body=%wide.region_5.6_spmd.clone.sunk | while | flops 132100 | bytes 332403 | solution.py:37
  171.1 0.9 add_select_fusion.4
  172.1 0.9 add_select_fusion.4
  173.1 0.9 add_select_fusion.4
  174.0 0.9 add_select_fusion.4
  175.0 0.9 add_select_fusion.4
  175.9 0.9 add_select_fusion.4
  176.9 0.9 add_select_fusion.4
  177.9 0.9 add_select_fusion.4
  178.8 0.9 add_select_fusion.4
  179.8 0.9 add_select_fusion.4
  180.8 0.9 add_select_fusion.4
  181.7 0.9 add_select_fusion.4
  182.7 0.9 add_select_fusion.4
  183.7 0.9 add_select_fusion.4
  184.6 0.9 add_select_fusion.4
  185.6 0.9 add_select_fusion.4
  186.6 0.9 add_select_fusion.4
  187.5 0.9 add_select_fusion.4
  188.5 0.9 add_select_fusion.4
  189.4 0.9 add_select_fusion.4
  190.4 0.9 add_select_fusion.4
  191.4 0.9 add_select_fusion.4
  192.3 0.9 add_select_fusion.4
  193.3 0.9 add_select_fusion.4
  194.3 0.9 add_select_fusion.4
  195.2 0.9 add_select_fusion.4
  196.2 0.9 add_select_fusion.4
  197.2 0.9 add_select_fusion.4
  198.1 0.9 add_select_fusion.4
  199.1 0.9 add_select_fusion.4
  200.1 0.9 add_select_fusion.4
  201.0 0.9 add_select_fusion.4
  202.0 58.0 %all-gather.8.cloned.1.call-done = bf16[16384,128]{1,0:T(8,128)(2,1)} async-done(((bf16[512,128]{1,0:T(8,128)(2,1)}), bf16[16384,128]{1,0:T(8,128)(2,1)}) %all-gather.8.cloned.1.call-update) | async-done | bytes 4194320 | tf_op jit(solution)/shard_map/all_gather | solution.py:65
  260.0 6.9 %convolution_convert_fusion.2 = bf16[256,128]{1,0:T(8,128)(2,1)S(1)} fusion(bf16[256,16384]{1,0:T(8,128)(2,1)} %param.8, bf16[16384,128]{1,0:T(8,128)(2,1)} %all-gather.8.cloned.1.call-done), kind=kOutput, calls=%fused_computation.15 | convolution fusion | flops 1073774592 | bytes 12648448 | tf_op jit(solution)/shard_map/dot_general | solution.py:63
  266.9 0.2 exponential_reduce_fusion.1
  267.2 0.2 fusion
  267.4 0.1 fusion.20
  267.6 0.4 fusion.32
  268.0 0.3 fusion.21
  268.3 1.2 fusion.6
  269.5 0.0 all-gather.10.cloned.1.call-update
  269.5 78.3 %all-gather.12.cloned.1.call-done = bf16[2048,1024]{1,0:T(8,128)(2,1)} async-done(((bf16[64,1024]{1,0:T(8,128)(2,1)}), bf16[2048,1024]{1,0:T(8,128)(2,1)}) %all-gather.12.cloned.1.call-update) | async-done | bytes 4194320 | tf_op jit(solution)/shard_map/all_gather | solution.py:123
  347.8 43.5 %all-gather.10.cloned.1.call-done = bf16[256,2048]{1,0:T(8,128)(2,1)} async-done(((bf16[256,128]{1,0:T(8,128)(2,1)}), bf16[256,2048]{1,0:T(8,128)(2,1)}) %all-gather.10.cloned.1.call-update) | async-done | bytes 1048592 | tf_op jit(solution)/shard_map/all_gather | solution.py:119
  391.3 4.6 %convolution_convert_fusion = bf16[256,1024]{1,0:T(8,128)(2,1)} fusion(bf16[256,2048]{1,0:T(8,128)(2,1)} %all-gather.10.cloned.1.call-done, bf16[2048,1024]{1,0:T(8,128)(2,1)} %all-gather.12.cloned.1.call-done), kind=kOutput, calls=%fused_computation.3 | convolution fusion | flops 1074003968 | bytes 5767168 | tf_op jit(solution)/shard_map/dot_general | solution.py:121
  (77 shorter events, 0.9 us)
Async XLA Ops:
  6.5 84.9 %copy-start = (bf16[128,128]{1,0:T(8,128)(2,1)S(1)}, bf16[128,128]{1,0:T(8,128)(2,1)}, u32[]{:S(2)}) copy-start(bf16[128,128]{1,0:T(8,128)(2,1)} %param.12) | copy-start | bytes 98308
  6.5 164.6 %all-gather.14.cloned.1.call-start = ((), (), s32[]{:S(2)}) async-start(), calls=%async_computation.3 | async-start | bytes 2162688 | tf_op jit(solution)/shard_map/all_gather | solution.py:20
  87.7 3.7 collective-permute-start
  93.1 166.9 %all-gather.8.cloned.1.call-start = ((), (), s32[]{:S(2)}) async-start(), calls=%async_computation | async-start | bytes 4325376 | tf_op jit(solution)/shard_map/all_gather | solution.py:65
  93.9 253.9 %all-gather.12.cloned.1.call-start = ((), (), s32[]{:S(2)}) async-start(), calls=%async_computation.2 | async-start | bytes 4325376 | tf_op jit(solution)/shard_map/all_gather | solution.py:123
  94.6 296.7 %all-gather.10.cloned.1.call-start = ((), (), s32[]{:S(2)}) async-start(), calls=%async_computation.1 | async-start | bytes 1114112 | tf_op jit(solution)/shard_map/all_gather | solution.py:119
  202.0 64.9 %copy-start.1 = (bf16[1,128,128]{2,1,0:T(8,128)(2,1)S(1)}, bf16[1,128,128]{2,1,0:T(8,128)(2,1)}, u32[]{:S(2)}) copy-start(bf16[1,128,128]{2,1,0:T(8,128)(2,1)} %param.11) | copy-start | bytes 98308
Sparse Core Ops, SparseCore 0:
  93.2 77.8 all-gather.13
  174.3 85.6 all-gather.7
  263.1 84.6 all-gather.11
  349.7 41.5 all-gather.9
where the time goes:
time: 404 us; the launch traced here: 402 us
  waiting for transfers between devices  224 us (55%)
  blocking collectives  111 us (27%)
  other arithmetic  30.2 us (7%)
  matrix products  21 us (5%)
  between operations  13.3 us (3%)
    all_gather x1, waiting for transfers between devices, per_device(): lax.all_gather(w_out, 'ctx', axis=0, tiled=True)  78.3 us
    all_gather x1, waiting for transfers between devices, per_device(): lax.all_gather(w_query, 'ctx', axis=0, tiled=True)  58 us
    all_gather x1, waiting for transfers between devices, per_device(): all_heads = lax.all_gather(attn_rows, 'head', axis=1, tiled=True)  43.5 us
    all_gather x1, waiting for transfers between devices, prefix(): lax.all_gather(part.astype(kind), axis)  41.1 us
    all_gather x1, blocking collectives, per_device(): lax.all_gather(w_keyval, 'ctx', axis=0, tiled=True)  39.9 us
    all_gather x1, blocking collectives, per_device(): lax.all_gather(pair_sum.astype(jnp.bfloat16), 'head', axis=1, tiled=True)  35.5 us
    all_gather x1, blocking collectives, prefix(): lax.all_gather(part.astype(kind), axis)  35.3 us
    select_n x64, other arithmetic, step(): return jax.tree.map(lambda a, b: jnp.where(reached, a, b), new, before)  29.3 us
  transfers between devices with their start and end apart: 5, of which 5 were waited for; matrix products, arithmetic and copies ran while one was open for 10% of the time, Pallas kernels for 0%

commit v1 on v0

v1 whole, which is shorter than its diff:
```python
import math

import jax
import jax.numpy as jnp
from jax import lax
from jax.experimental import pallas as pl
from jax.experimental.pallas import tpu as pltpu
from jax.sharding import PartitionSpec as P

WINDOW = 64
NX = 4
CORES = 2
SUBS = 2
MESH = pl.DeviceIdType.MESH
F32 = jnp.float32
BF16 = jnp.bfloat16


def rem(a, b):
    return lax.rem(a, jnp.int32(b))


def div(a, b):
    return lax.div(a, jnp.int32(b))


def ring_pos(cycle, y, x, ny):
    if cycle == 0:
        return NX * y + rem(x + y, NX)
    t = rem(y + 3 * ny - 3 * x, ny)
    return 4 * (x + NX * div(t, 4)) + rem(t, 4)


def ring_node(cycle, s, ny):
    a, b = div(s, 4), rem(s, 4)
    if cycle == 0:
        y, x = a, rem(b + 4 * ny - a, NX)
    else:
        y, x = rem(3 * a + b, ny), rem(a, NX)
    return NX * y + x


def features(logits, axis):
    rising = jnp.exp(logits)
    falling = jnp.exp(-logits)
    rising = rising / jnp.sum(rising, axis=axis, keepdims=True)
    falling = falling / jnp.sum(falling, axis=axis, keepdims=True)
    return jnp.concatenate([rising, falling], axis=axis).astype(BF16)


def remote(src, dst, send_sem, recv_sem, ctx, head):
    return pltpu.make_async_remote_copy(
        src_ref=src,
        dst_ref=dst,
        send_sem=send_sem,
        recv_sem=recv_sem,
        device_id={"ctx": ctx, "head": head},
        device_id_type=MESH,
    )


def sublayer_kernel(
    nctx,
    nhead,
    x_hbm,
    wq_hbm,
    wkv_ref,
    fq_ref,
    fk_ref,
    wo_hbm,
    out_ref,
    xbuf,
    wbuf,
    mask,
    acc,
    wfull,
    kvall,
    bord,
    kfbuf,
    stx,
    sty,
    mz,
    attn,
    oacc,
    xsem,
    lsem,
    q_send,
    q_recv,
    o_send,
    o_recv,
    kv_recv,
    b_recv,
    x_recv,
    y_recv,
    m_recv,
    z_recv,
    s_recv,
    misc_send,
):
    ny, nz = nctx // NX, nhead // CORES
    hops = nctx // 2
    zhops = nz // 2
    c = lax.axis_index("ctx")
    h = lax.axis_index("head")
    y, x = div(c, NX), rem(c, NX)
    z, core = div(h, CORES), rem(h, CORES)
    tokens = x_hbm.shape[0]
    half = wq_hbm.shape[0] // 2
    ohalf = wo_hbm.shape[0] // 2
    packed = half // 8
    rows = half + packed
    dim = fk_ref.shape[0]
    width = wkv_ref.shape[1]
    sibling = CORES * z + 1 - core

    place = [ring_pos(k, y, x, ny) for k in range(2)]
    ahead = [ring_node(k, rem(place[k] + 1, nctx), ny) for k in range(2)]
    behind = [ring_node(k, rem(place[k] + nctx - 1, nctx), ny) for k in range(2)]
    target = [ahead[0], behind[0], ahead[1], behind[1]]
    limit = [hops, hops - 1, hops, hops - 1]

    def owner(stream, k):
        cycle = stream // 2
        if stream % 2 == 0:
            return ring_node(cycle, rem(place[cycle] + 2 * nctx - 1 - k, nctx), ny)
        return ring_node(cycle, rem(place[cycle] + 1 + k, nctx), ny)

    barrier = pltpu.get_barrier_semaphore()

    def greet(ctx, head):
        pl.semaphore_signal(
            barrier, inc=1, device_id={"ctx": ctx, "head": head}, device_id_type=MESH
        )

    for ctx in target:
        greet(ctx, h)
    for j in range(1, NX):
        greet(NX * y + rem(x + j, NX), h)

    @pl.loop(1, ny)
    def _(j):
        greet(NX * rem(y + j, ny) + x, h)

    @pl.loop(1, nhead)
    def _(j):
        greet(c, rem(h + j, nhead))

    following, previous = rem(c + 1, nctx), rem(c + nctx - 1, nctx)
    greet(following, h)
    greet(previous, h)

    own_q = [
        pltpu.make_async_copy(
            wq_hbm.at[pl.ds(half * k, half)],
            wbuf.at[c, k, pl.ds(0, half)],
            lsem.at[k],
        )
        for k in range(2)
    ]
    own_o = [
        pltpu.make_async_copy(
            wo_hbm.at[pl.ds(ohalf * k, ohalf)], wfull.at[c, k], lsem.at[2 + k]
        )
        for k in range(2)
    ]
    for copy in own_q:
        copy.start()

    @pl.loop(0, 2 * nctx)
    def _(j):
        pltpu.make_async_copy(
            x_hbm.at[:, pl.ds(pl.multiple_of(j * half, half), half)], xbuf.at[j], xsem
        ).start()

    for copy in own_o:
        copy.start()

    row_id = lax.broadcasted_iota(jnp.int32, (half, 8 * width), 0)
    lane_id = lax.broadcasted_iota(jnp.int32, (half, 8 * width), 1)
    group = jnp.where(div(row_id, packed) == div(lane_id, width), 1.0, 0.0)
    mask[...] = group.astype(BF16)
    spread = jnp.where(
        lax.broadcasted_iota(jnp.int32, (width, 8 * width), 0)
        == rem(lax.broadcasted_iota(jnp.int32, (width, 8 * width), 1), width),
        1.0,
        0.0,
    ).astype(BF16)
    for k in range(2):
        wide = jnp.dot(
            wkv_ref[pl.ds(half * k, half), :], spread, preferred_element_type=F32
        )
        wide = wide * group
        dense = wide[:packed]
        for j in range(1, 8):
            dense = dense + wide[packed * j : packed * (j + 1)]
        wbuf[c, k, pl.ds(half, packed)] = dense.astype(BF16)

    pl.semaphore_wait(barrier, 4 + (NX - 1) + (ny - 1) + (nhead - 1) + 2)

    piece = rows // SUBS

    def q_copy(stream, k, sub, block):
        part = wbuf.at[block, stream // 2, pl.ds(piece * sub, piece)]
        return remote(
            part, part, q_send.at[stream], q_recv.at[stream, k, sub], target[stream], h
        )

    for copy in own_q:
        copy.wait()
    for sub in range(SUBS):
        for stream in range(4):
            q_copy(stream, 0, sub, c).start()

    def product(block, k):
        part = wbuf[block, k]
        wide = jnp.concatenate([part[half:]] * 8, axis=0) * mask[...]
        weights = jnp.concatenate([part[:half], wide], axis=1)
        return jnp.dot(xbuf[2 * block + k], weights, preferred_element_type=F32)

    pltpu.make_async_copy(xbuf, xbuf, xsem).wait()
    acc[...] = product(c, 0) + product(c, 1)

    def q_step(k, receiving, sending):
        blocks = [owner(stream, k) for stream in range(4)]
        for sub in range(SUBS):
            for stream in receiving:
                q_copy(stream, k, sub, blocks[stream]).wait_recv()
                if stream in sending:
                    q_copy(stream, k + 1, sub, blocks[stream]).start()
        total = product(blocks[receiving[0]], receiving[0] // 2)
        for stream in receiving[1:]:
            total = total + product(blocks[stream], stream // 2)
        acc[...] += total

    @pl.loop(0, hops - 2)
    def _(k):
        q_step(k, (0, 1, 2, 3), (0, 1, 2, 3))

    q_step(jnp.int32(hops - 2), (0, 1, 2, 3), (0, 2))

    opiece = ohalf // SUBS

    def o_copy(stream, k, sub, block):
        part = wfull.at[block, stream // 2, pl.ds(opiece * sub, opiece)]
        return remote(
            part, part, o_send.at[stream], o_recv.at[stream, k, sub], target[stream], h
        )

    def o_step(k, receiving, sending):
        for sub in range(SUBS):
            for stream in receiving:
                block = owner(stream, k)
                o_copy(stream, k, sub, block).wait_recv()
                if stream in sending:
                    o_copy(stream, k + 1, sub, block).start()

    def o_steps(first, last):
        if first < min(last, hops - 2):

            @pl.loop(first, min(last, hops - 2))
            def _(k):
                o_step(k, (0, 1, 2, 3), (0, 1, 2, 3))

        if first <= hops - 2 < last:
            o_step(jnp.int32(hops - 2), (0, 1, 2, 3), (0, 2))
        if first <= hops - 1 < last:
            o_step(jnp.int32(hops - 1), (0, 2), ())

    for copy in own_o:
        copy.wait()
    for sub in range(SUBS):
        for stream in range(4):
            o_copy(stream, 0, sub, c).start()

    q_step(jnp.int32(hops - 1), (0, 2), ())

    queries = acc[:, :dim].astype(BF16)
    folded = acc[:, dim:].T
    own_kv = folded[:width]
    for j in range(1, 8):
        own_kv = own_kv + folded[width * j : width * (j + 1)]
    kvall[h] = own_kv.astype(BF16)

    def to_heads(buffer, sems, send):
        @pl.loop(1, nhead)
        def _(j):
            remote(
                buffer.at[h], buffer.at[h], send, sems.at[h], c, rem(h + j, nhead)
            ).start()

    def from_heads(buffer, sems, send):
        @pl.loop(1, nhead)
        def _(j):
            source = rem(h + j, nhead)
            remote(
                buffer.at[source], buffer.at[source], send, sems.at[source], c, source
            ).wait_recv()

    to_heads(kvall, kv_recv, misc_send.at[0])

    query_feats = features(
        jnp.dot(queries, fq_ref[0], preferred_element_type=F32), 1
    )
    o_steps(0, 2)

    from_heads(kvall, kv_recv, misc_send.at[0])
    edge = tokens - 2 * WINDOW
    border = remote(
        kvall.at[:, :, pl.ds(edge, 2 * WINDOW)],
        bord,
        misc_send.at[1],
        b_recv,
        following,
        h,
    )
    border.start()
    o_steps(2, 3)
    border.wait_recv()

    both = jnp.concatenate([bord[...], kvall[...]], axis=2)
    extent = tokens + 2 * WINDOW
    both = both.reshape(2 * dim, extent)
    keys, values = both[:dim], both[dim:]
    fk_t = fk_ref[...].astype(F32).T.astype(BF16)
    key_feats = features(jnp.dot(fk_t, keys, preferred_element_type=F32), 0)
    kfbuf[...] = key_feats.reshape(nhead, 2 * dim // nhead, extent)
    lowest = jnp.where(c > 0, WINDOW, 2 * WINDOW)
    mine = kfbuf[h].astype(F32)
    lane = lax.broadcasted_iota(jnp.int32, mine.shape, 1)
    mine = jnp.where((lane >= lowest) & (lane < extent - WINDOW), mine, 0.0)
    stx[x, 0] = lax.dot_general(
        mine.astype(BF16), values, (((1,), (1,)), ((), ())), preferred_element_type=F32
    )
    stx[x, 1] = jnp.broadcast_to(
        jnp.sum(mine, axis=1, keepdims=True), (mine.shape[0], dim)
    )
    for j in range(1, NX):
        remote(
            stx.at[x],
            stx.at[x],
            misc_send.at[2],
            x_recv.at[x],
            NX * y + rem(x + j, NX),
            h,
        ).start()
    o_steps(3, 5)

    for j in range(1, NX):
        source = rem(x + j, NX)
        remote(
            stx.at[source],
            stx.at[source],
            misc_send.at[2],
            x_recv.at[source],
            NX * y + source,
            h,
        ).wait_recv()
    row = stx[0] + stx[1] + stx[2] + stx[3]
    before = jnp.zeros_like(row)
    for j in range(NX - 1):
        before = before + stx[j] * jnp.where(j < x, 1.0, 0.0)
    sty[y] = row

    @pl.loop(1, ny)
    def _(j):
        remote(
            sty.at[y],
            sty.at[y],
            misc_send.at[3],
            y_recv.at[y],
            NX * rem(y + j, ny) + x,
            h,
        ).start()

    o_steps(5, 6)

    token = lax.broadcasted_iota(jnp.int32, (tokens, extent), 0)
    key_at = lax.broadcasted_iota(jnp.int32, (tokens, extent), 1)
    offset = token + 2 * WINDOW - key_at
    held = key_at >= lowest
    inside = (offset >= 0) & (offset < WINDOW) & held
    beyond = (offset >= WINDOW) & held
    scores = jnp.dot(queries, keys, preferred_element_type=F32) * (1.0 / math.sqrt(dim))
    far = jnp.dot(query_feats, key_feats, preferred_element_type=F32)
    weights = jnp.where(inside, jnp.exp(scores), 0.0) + jnp.where(beyond, far, 0.0)
    numerator = lax.dot_general(
        weights.astype(BF16),
        values,
        (((1,), (1,)), ((), ())),
        preferred_element_type=F32,
    )
    denominator = jnp.sum(weights, axis=1, keepdims=True)
    o_steps(6, 7)

    @pl.loop(1, ny)
    def _(j):
        source = rem(y + j, ny)
        remote(
            sty.at[source],
            sty.at[source],
            misc_send.at[3],
            y_recv.at[source],
            NX * source + x,
            h,
        ).wait_recv()

    for j in range(ny - 1):
        before = before + sty[j] * jnp.where(j < y, 1.0, 0.0)
    mz[h] = before.astype(BF16)
    to_heads(mz, m_recv, misc_send.at[4])
    o_steps(7, 9)
    from_heads(mz, m_recv, misc_send.at[4])
    matrix = mz[:, 0].reshape(2 * dim, dim)
    totals = mz[:, 1].reshape(2 * dim, dim)
    numerator = numerator + jnp.dot(query_feats, matrix, preferred_element_type=F32)
    denominator = denominator + jnp.dot(query_feats, totals, preferred_element_type=F32)
    attn[z, core] = (numerator / denominator).astype(BF16)

    zlimit = [zhops, zhops - 1]
    ztarget = [
        CORES * rem(z + 1, nz) + core,
        CORES * rem(z + nz - 1, nz) + core,
    ]
    tpiece = tokens // SUBS

    def z_source(stream, k):
        if stream == 0:
            return rem(z + 2 * nz - 1 - k, nz)
        return rem(z + 1 + k, nz)

    def z_copy(stream, k, sub, block):
        part = attn.at[block, core, pl.ds(tpiece * sub, tpiece)]
        return remote(
            part, part, misc_send.at[5 + stream], z_recv.at[stream, k, sub], c, ztarget[stream]
        )

    def to_sibling(block):
        remote(
            attn.at[block, core],
            attn.at[block, core],
            misc_send.at[7],
            s_recv.at[block],
            c,
            sibling,
        ).start()

    def from_sibling(block):
        remote(
            attn.at[block, 1 - core],
            attn.at[block, 1 - core],
            misc_send.at[7],
            s_recv.at[block],
            c,
            sibling,
        ).wait_recv()

    def z_step(k):
        streams = [s for s in range(2) if k < zlimit[s]]
        for sub in range(SUBS):
            for s in streams:
                block = z_source(s, k)
                z_copy(s, k, sub, block).wait_recv()
                if k + 1 < zlimit[s]:
                    z_copy(s, k + 1, sub, block).start()
        for s in streams:
            to_sibling(z_source(s, k))

    for sub in range(SUBS):
        for s in range(2):
            if zlimit[s]:
                z_copy(s, 0, sub, z).start()
    to_sibling(z)
    done = 9
    for k in range(zhops):
        upto = min(hops, done + 2) if k < zhops - 1 else hops
        o_steps(done, upto)
        done = upto
        z_step(k)

    def out_product(block):
        heads = jnp.concatenate([attn[block, 0], attn[block, 1]], axis=1)
        weights = wfull[pl.ds(2 * CORES * block, 2 * CORES)].reshape(
            CORES * dim, wo_hbm.shape[1]
        )
        return jnp.dot(heads, weights, preferred_element_type=F32)

    from_sibling(z)
    oacc[...] = out_product(z)
    for k in range(zhops):
        for s in range(2):
            if k < zlimit[s]:
                block = z_source(s, k)
                from_sibling(block)
                oacc[...] += out_product(block)
    out_ref[...] = oacc[...].astype(BF16)

    def sent(ref, sem):
        remote(ref, ref, sem, b_recv, following, h).wait_send()

    for stream in range(4):
        sent(wbuf.at[pl.ds(0, limit[stream]), 0], q_send.at[stream])
        sent(wfull.at[pl.ds(0, limit[stream]), 0], o_send.at[stream])
    sent(kvall.at[pl.ds(0, nhead - 1)], misc_send.at[0])
    sent(bord, misc_send.at[1])
    sent(stx.at[pl.ds(0, NX - 1)], misc_send.at[2])
    sent(sty.at[pl.ds(0, ny - 1)], misc_send.at[3])
    sent(mz.at[pl.ds(0, nhead - 1)], misc_send.at[4])
    for s in range(2):
        if zlimit[s]:
            sent(attn.at[pl.ds(0, zlimit[s]), 0], misc_send.at[5 + s])
    sent(attn.at[:, 0], misc_send.at[7])


def per_device(activations, w_query, w_keyval, f_query, f_key, w_out):
    nctx, nhead = lax.axis_size("ctx"), lax.axis_size("head")
    ny, nz = nctx // NX, nhead // CORES
    hops = nctx // 2
    tokens = activations.shape[0]
    half, ohalf = w_query.shape[0] // 2, w_out.shape[0] // 2
    dim, columns = f_key.shape[0], w_out.shape[1]
    width = w_keyval.shape[1]
    extent = tokens + 2 * WINDOW
    part = 2 * dim // nhead

    def kernel(*refs):
        sublayer_kernel(nctx, nhead, *refs)

    dma = pltpu.SemaphoreType.DMA
    anywhere = pl.BlockSpec(memory_space=pl.ANY)
    vmem = pl.BlockSpec(memory_space=pltpu.VMEM)
    return pl.pallas_call(
        kernel,
        out_shape=jax.ShapeDtypeStruct((tokens, columns), BF16),
        in_specs=[anywhere, anywhere, vmem, vmem, vmem, anywhere],
        out_specs=vmem,
        scratch_shapes=[
            pltpu.VMEM((2 * nctx, tokens, half), BF16),
            pltpu.VMEM((nctx, 2, half + half // 8, dim), BF16),
            pltpu.VMEM((half, 8 * width), BF16),
            pltpu.VMEM((tokens, dim + 8 * width), F32),
            pltpu.VMEM((nctx, 2, ohalf, columns), BF16),
            pltpu.VMEM((nhead, width, tokens), BF16),
            pltpu.VMEM((nhead, width, 2 * WINDOW), BF16),
            pltpu.VMEM((nhead, part, extent), BF16),
            pltpu.VMEM((NX, 2, part, dim), F32),
            pltpu.VMEM((ny, 2, part, dim), F32),
            pltpu.VMEM((nhead, 2, part, dim), BF16),
            pltpu.VMEM((nz, CORES, tokens, dim), BF16),
            pltpu.VMEM((tokens, columns), F32),
            dma,
            dma((4,)),
            dma((4,)),
            dma((4, hops, SUBS)),
            dma((4,)),
            dma((4, hops, SUBS)),
            dma((nhead,)),
            dma,
            dma((NX,)),
            dma((ny,)),
            dma((nhead,)),
            dma((2, max(nz // 2, 1), SUBS)),
            dma((nz,)),
            dma((8,)),
        ],
        compiler_params=pltpu.CompilerParams(
            collective_id=0, has_side_effects=True, vmem_limit_bytes=56 << 20
        ),
    )(activations, w_query, w_keyval, f_query, f_key, w_out)


def solution(mesh):
    in_specs = (
        P("ctx", None),
        P("ctx", "head"),
        P("ctx", "head"),
        P("head", None, None),
        P(),
        P("ctx", "head"),
    )
    out_specs = P("ctx", "head")
    return jax.shard_map(
        per_device, mesh=mesh, in_specs=in_specs, out_specs=out_specs, check_vma=False
    )
```

time: 404 us -> 137 us (0.34)
  waiting for transfers between devices: 224 us -> 0 us
  Pallas kernels: 0 us -> 133 us
  blocking collectives: 111 us -> 0 us
  other arithmetic: 30.2 us -> 0 us
  matrix products: 21 us -> 0 us
  between operations: 13.3 us -> 0.01 us
    all_gather x4 -> x0, waiting for transfers between devices: 221 us -> none  [the longest x1 78.3 us: per_device(): lax.all_gather(w_out, 'ctx', axis=0, tiled=True)]
    pallas_call x0 -> x1, Pallas kernels: none -> 133 us  [per_device(): pl.pallas_call(kernel, out_shape=jax.ShapeDtypeStruct((tokens, columns),...]
    all_gather x3 -> x0, blocking collectives: 111 us -> none  [the longest x1 39.9 us: per_device(): lax.all_gather(w_keyval, 'ctx', axis=0, tiled=True)]
    select_n x65 -> x0, other arithmetic: 29.5 us -> none  [the longest x64 29.3 us: step(): return jax.tree.map(lambda a, b: jnp.where(reached, a, b), new, before)]
    dot_general x11 -> x0, matrix products: 21 us -> none  [the longest x1 6.91 us: per_device(): jnp.dot(columns, lax.all_gather(w_query, 'ctx', axis=0, tiled=True), pref...]
  transfers between devices with their start and end apart: 5 -> 0, of which waited for: 5 -> 0; matrix products, arithmetic and copies ran while one was open for 10% -> 0% of each run, Pallas kernels for 0% -> 0%
where the time goes in v1:
time: 137 us
  Pallas kernels  133 us (97%)
  local copies, waits for them, and re-layouts  3.34 us (2%)
    pallas_call x1, Pallas kernels, per_device(): pl.pallas_call(kernel, out_shape=jax.ShapeDtypeStruct((tokens, columns),...  133 us
    unnamed x2, local copies, waits for them, and re-layouts  3.34 us

profile of v1, /device:TPU:1, one launch (start us, length us, event | category | flops | bytes accessed | tf_op | source)
XLA Modules:
  0.0 136.6 jit_solution(6110311720400905475)
XLA Ops:
  0.0 1.5 %copy.7.refs_2_ = bf16[512,16]{1,0:T(8,128)(2,1)} copy(bf16[512,16]{0,1:T(8,128)(2,1)} %param.8) | data formatting | bytes 32768 | tf_op args[2]
  1.5 133.2 %shard_map.64 = bf16[256,1024]{1,0:T(8,128)(2,1)} custom-call(bf16[256,16384]{1,0:T(8,128)(2,1)} %refs_0_.1, bf16[512,128]{1,0:T(8,128)(2,1)} %refs_1_.1, bf16[512,16]{1,0:T(8,128)(2,1)} %copy.7.refs_2_, bf16[1,128,128]{2,1,0:T(8,128)(2,1)} %refs_3_.1, bf16[128,128]{1,0:T(8,128)(2,1)} %refs_4_.1, bf16[64,1024]{1,0:T(8,128)(2,1)} %refs_5_.1), custom_call_target="tpu_custom_call" | custom-call | tf_op jit(solution)/shard_map/pallas_call | solution.py:531
  134.7 1.9 %copy.9 = bf16[256,1024]{1,0:T(8,128)(2,1)} copy(bf16[256,1024]{1,0:T(8,128)(2,1)} %shard_map.64) | data formatting | bytes 1048576

commit v2 on v1

v2 whole, which is shorter than its diff:
```python
import math

import jax
import jax.numpy as jnp
from jax import lax
from jax.experimental import pallas as pl
from jax.experimental.pallas import tpu as pltpu
from jax.sharding import PartitionSpec as P

WINDOW = 64
NX = 4
CORES = 2
MESH = pl.DeviceIdType.MESH
F32 = jnp.float32
BF16 = jnp.bfloat16


def rem(a, b):
    return lax.rem(a, jnp.int32(b))


def div(a, b):
    return lax.div(a, jnp.int32(b))


def features(logits, axis):
    rising = jnp.exp(logits)
    falling = jnp.exp(-logits)
    rising = rising / jnp.sum(rising, axis=axis, keepdims=True)
    falling = falling / jnp.sum(falling, axis=axis, keepdims=True)
    return jnp.concatenate([rising, falling], axis=axis).astype(BF16)


def remote(src, dst, send_sem, recv_sem, ctx, head):
    return pltpu.make_async_remote_copy(
        src_ref=src,
        dst_ref=dst,
        send_sem=send_sem,
        recv_sem=recv_sem,
        device_id={"ctx": ctx, "head": head},
        device_id_type=MESH,
    )


class Spread:
    def __init__(self, size, place, block, device, send_sem, recv_sem):
        self.size, self.place = size, place
        self.block, self.device = block, device
        self.send_sem, self.recv_sem = send_sem, recv_sem

    def at(self, offset):
        return rem(self.place + offset + self.size, self.size)

    def copy(self, source, offset):
        part = self.block(source)
        return remote(
            part,
            part,
            self.send_sem,
            self.recv_sem.at[source],
            *self.device(self.at(offset)),
        )

    def start(self):
        for offset in (1, -1, 2, -2):
            self.copy(self.place, offset).start()

    def wait(self, offset):
        self.copy(self.at(offset), 1).wait_recv()

    def forward_up(self):
        self.copy(self.at(-2), 1).start()
        self.copy(self.at(-2), 2).start()

    def forward_down(self):
        self.copy(self.at(2), -1).start()


class Gather:
    def __init__(self, buffer, y, x, ny, h, send, ax, ay, by, bx):
        self.buffer, self.y, self.x, self.ny, self.h = buffer, y, x, ny, h
        self.send, self.ax, self.ay, self.bx = send, ax, ay, bx
        self.b = Spread(
            ny,
            y,
            lambda source: buffer.at[NX * source + x, 1],
            lambda place: (NX * place + x, h),
            send.at[1],
            by,
        )

    def ring(self, offset):
        return rem(self.y + offset + self.ny, self.ny)

    def a_copy_x(self, source, to):
        part = self.buffer.at[NX * self.y + source, 0]
        return remote(
            part, part, self.send.at[0], self.ax.at[source], NX * self.y + to, self.h
        )

    def a_start(self):
        for j in range(1, NX):
            self.a_copy_x(self.x, rem(self.x + j, NX)).start()

    def a_wait(self):
        for j in range(1, NX):
            self.a_copy_x(rem(self.x + j, NX), self.x).wait_recv()

    def a_sets(self, k):
        last = k == self.ny // 2 - 1
        return [
            (way, col)
            for col in range(NX)
            for way in range(2)
            if not last or (way == 0) == (col < NX // 2)
        ]

    def a_source(self, way, k):
        return self.ring(-(k + 1) if way == 0 else k + 1)

    def a_copy(self, way, k, col, row):
        part = self.buffer.at[NX * row + col, 0]
        to = self.ring(1 if way == 0 else -1)
        return remote(
            part,
            part,
            self.send.at[0],
            self.ay.at[way, k, col],
            NX * to + self.x,
            self.h,
        )

    def a_first(self):
        for way, col in self.a_sets(0):
            self.a_copy(way, 0, col, self.y).start()

    def a_hop(self, k):
        onward = self.a_sets(k + 1) if k + 1 < self.ny // 2 else []
        for way, col in self.a_sets(k):
            row = self.a_source(way, k)
            self.a_copy(way, k, col, row).wait_recv()
            if (way, col) in onward:
                self.a_copy(way, k + 1, col, row).start()
        return [(self.a_source(way, k), col) for way, col in self.a_sets(k)]

    def b_copy_x(self, row, source, to):
        part = self.buffer.at[NX * row + source, 1]
        return remote(
            part, part, self.send.at[1], self.bx.at[row, source], NX * self.y + to, self.h
        )

    def b_along_x(self, offset):
        row = self.ring(offset)
        for j in range(1, NX):
            self.b_copy_x(row, self.x, rem(self.x + j, NX)).start()

    def b_near(self):
        for offset in (-1, 1):
            self.b.wait(offset)
            self.b_along_x(offset)
        self.b.wait(-2)
        self.b.forward_up()
        self.b_along_x(-2)
        self.b.wait(2)
        self.b.forward_down()
        self.b_along_x(2)

    def b_far(self):
        for offset in (-3, 3, -4):
            self.b.wait(offset)
            self.b_along_x(offset)

    def b_wait_x(self, offset):
        row = self.ring(offset)
        for j in range(1, NX):
            self.b_copy_x(row, rem(self.x + j, NX), self.x).wait_recv()
        return [(row, col) for col in range(NX)]

    def finish(self, sent):
        count = NX * self.ny - 1
        for k in range(2):
            sent(self.buffer.at[pl.ds(0, count), k], self.send.at[k])


def sublayer_kernel(
    nctx,
    nhead,
    x_hbm,
    wq_hbm,
    wkv_ref,
    fq_ref,
    fk_ref,
    wo_hbm,
    out_ref,
    xbuf,
    wbuf,
    wkv,
    acc,
    wfull,
    kvall,
    bord,
    kfbuf,
    stx,
    sty,
    mz,
    attn,
    xsem,
    lsem,
    q_send,
    q_ax,
    q_ay,
    q_by,
    q_bx,
    o_send,
    o_ax,
    o_ay,
    o_by,
    o_bx,
    w_x,
    w_y,
    kv_recv,
    b_recv,
    x_recv,
    y_recv,
    m_recv,
    z_recv,
    s_recv,
    misc_send,
):
    ny, nz = nctx // NX, nhead // CORES
    c = lax.axis_index("ctx")
    h = lax.axis_index("head")
    y, x = div(c, NX), rem(c, NX)
    z, core = div(h, CORES), rem(h, CORES)
    tokens = x_hbm.shape[0]
    half = wq_hbm.shape[0] // 2
    ohalf = wo_hbm.shape[0] // 2
    dim = fk_ref.shape[0]
    sibling = CORES * z + 1 - core
    following, previous = rem(c + 1, nctx), rem(c + nctx - 1, nctx)

    barrier = pltpu.get_barrier_semaphore()

    def greet(ctx, head):
        pl.semaphore_signal(
            barrier, inc=1, device_id={"ctx": ctx, "head": head}, device_id_type=MESH
        )

    for j in range(1, NX):
        greet(NX * y + rem(x + j, NX), h)

    @pl.loop(1, ny)
    def _(j):
        greet(NX * rem(y + j, ny) + x, h)

    @pl.loop(1, nhead)
    def _(j):
        greet(c, rem(h + j, nhead))

    greet(following, h)
    greet(previous, h)

    own_q = [
        pltpu.make_async_copy(
            wq_hbm.at[pl.ds(half * k, half)], wbuf.at[c, k], lsem.at[k]
        )
        for k in range(2)
    ]
    own_o = [
        pltpu.make_async_copy(
            wo_hbm.at[pl.ds(ohalf * k, ohalf)], wfull.at[c, k], lsem.at[2 + k]
        )
        for k in range(2)
    ]
    for copy in own_q:
        copy.start()

    @pl.loop(0, 2 * nctx)
    def _(j):
        pltpu.make_async_copy(
            x_hbm.at[:, pl.ds(pl.multiple_of(j * half, half), half)], xbuf.at[j], xsem
        ).start()

    for copy in own_o:
        copy.start()
    wkv[y, x] = wkv_ref[...]

    pl.semaphore_wait(barrier, (NX - 1) + (ny - 1) + (nhead - 1) + 2)

    q = Gather(wbuf, y, x, ny, h, q_send, q_ax, q_ay, q_by, q_bx)
    o = Gather(wfull, y, x, ny, h, o_send, o_ax, o_ay, o_by, o_bx)
    w = Spread(
        ny,
        y,
        lambda source: wkv.at[source],
        lambda place: (NX * place + x, h),
        misc_send.at[8],
        w_y,
    )

    def w_copy_x(source, to):
        part = wkv.at[y, source]
        return remote(part, part, misc_send.at[9], w_x.at[source], NX * y + to, h)

    for j in range(1, NX):
        w_copy_x(x, rem(x + j, NX)).start()
    for copy in own_q:
        copy.wait()
    q.a_start()
    q.b.start()
    for j in range(1, NX):
        w_copy_x(rem(x + j, NX), x).wait_recv()
    w.start()
    q.a_wait()
    q.a_first()
    q.b_along_x(0)

    def q_product(pairs, k):
        total = None
        for row, col in pairs:
            block = NX * row + col
            term = jnp.dot(
                xbuf[2 * block + k], wbuf[block, k], preferred_element_type=F32
            )
            total = term if total is None else total + term
        return total

    pltpu.make_async_copy(xbuf, xbuf, xsem).wait()
    acc[...] = q_product([(y, col) for col in range(NX)], 0)
    q.b_near()
    for offset in (-1, 1):
        w.wait(offset)
    w.wait(-2)
    w.forward_up()
    w.wait(2)
    w.forward_down()
    pairs0 = q.a_hop(0)
    for offset in (-3, 3, -4):
        w.wait(offset)

    contract_last = (((1,), (1,)), ((), ()))

    def kv_step(block, total):
        part = wkv[div(block, NX), rem(block, NX)]
        for k in range(2):
            total = total + lax.dot_general(
                part[:, half * k : half * (k + 1)],
                xbuf[2 * block + k],
                contract_last,
                preferred_element_type=F32,
            )
        return total

    own_kv = lax.fori_loop(
        0, nctx, kv_step, jnp.zeros((wkv.shape[2], tokens), F32), unroll=4
    )
    kvall[h] = own_kv.astype(BF16)

    def to_heads(buffer, sems, send):
        @pl.loop(1, nhead)
        def _(j):
            remote(
                buffer.at[h], buffer.at[h], send, sems.at[h], c, rem(h + j, nhead)
            ).start()

    def from_heads(buffer, sems, send):
        @pl.loop(1, nhead)
        def _(j):
            source = rem(h + j, nhead)
            remote(
                buffer.at[source], buffer.at[source], send, sems.at[source], c, source
            ).wait_recv()

    to_heads(kvall, kv_recv, misc_send.at[0])
    q.b_far()
    pairs1 = q.a_hop(1)
    acc[...] += q_product(pairs0, 0)
    acc[...] += q_product(q.b_wait_x(0), 1)

    from_heads(kvall, kv_recv, misc_send.at[0])
    border = remote(
        kvall.at[:, :, pl.ds(tokens - 2 * WINDOW, 2 * WINDOW)],
        bord,
        misc_send.at[1],
        b_recv,
        following,
        h,
    )
    border.start()
    own = kvall[...].reshape(2 * dim, tokens)
    fk_t = fk_ref[...].astype(F32).T.astype(BF16)
    own_feats = features(jnp.dot(fk_t, own[:dim], preferred_element_type=F32), 0)
    part = 2 * dim // nhead
    edge = 2 * WINDOW
    kfbuf[:, :, edge:] = own_feats.reshape(nhead, part, tokens)

    def state(feats, values):
        matrix = lax.dot_general(
            feats, values, contract_last, preferred_element_type=F32
        )
        total = jnp.sum(feats.astype(F32), axis=1, keepdims=True)
        return matrix, jnp.broadcast_to(total, (part, dim))

    matrix, total = state(kfbuf[h, :, edge:], own[dim:])
    stx[x, 0] = matrix
    stx[x, 1] = total
    for j in range(1, NX):
        remote(
            stx.at[x],
            stx.at[x],
            misc_send.at[2],
            x_recv.at[x],
            NX * y + rem(x + j, NX),
            h,
        ).start()

    pairs2 = q.a_hop(2)
    acc[...] += q_product(pairs1, 0)
    for offset in (-1, 1):
        acc[...] += q_product(q.b_wait_x(offset), 1)

    for j in range(1, NX):
        source = rem(x + j, NX)
        remote(
            stx.at[source],
            stx.at[source],
            misc_send.at[2],
            x_recv.at[source],
            NX * y + source,
            h,
        ).wait_recv()
    row = stx[0] + stx[1] + stx[2] + stx[3]
    before = jnp.zeros_like(row)
    for j in range(NX - 1):
        before = before + stx[j] * jnp.where(j < x, 1.0, 0.0)
    sty[y] = row

    @pl.loop(1, ny)
    def _(j):
        remote(
            sty.at[y],
            sty.at[y],
            misc_send.at[3],
            y_recv.at[y],
            NX * rem(y + j, ny) + x,
            h,
        ).start()

    for copy in own_o:
        copy.wait()
    o.a_start()
    o.b.start()
    acc[...] += q_product(pairs2, 0)
    for offset in (-2, 2, -3):
        acc[...] += q_product(q.b_wait_x(offset), 1)
    pairs3 = q.a_hop(3)
    o.a_wait()
    o.a_first()
    o.b_along_x(0)
    for offset in (3, -4):
        acc[...] += q_product(q.b_wait_x(offset), 1)
    acc[...] += q_product(pairs3, 0)
    queries = acc[...].astype(BF16)
    query_feats = features(jnp.dot(queries, fq_ref[0], preferred_element_type=F32), 1)
    o.b_near()

    border.wait_recv()
    edge_kv = bord[...].reshape(2 * dim, edge)
    edge_feats = features(jnp.dot(fk_t, edge_kv[:dim], preferred_element_type=F32), 0)
    kfbuf[:, :, :edge] = edge_feats.reshape(nhead, part, edge)
    lowest = jnp.where(c > 0, WINDOW, edge)
    mine = kfbuf[h, :, :edge].astype(F32)
    held = lax.broadcasted_iota(jnp.int32, mine.shape, 1) >= lowest
    matrix, total = state(jnp.where(held, mine, 0.0).astype(BF16), edge_kv[dim:])

    @pl.loop(1, ny)
    def _(j):
        source = rem(y + j, ny)
        remote(
            sty.at[source],
            sty.at[source],
            misc_send.at[3],
            y_recv.at[source],
            NX * source + x,
            h,
        ).wait_recv()

    for j in range(ny - 1):
        before = before + sty[j] * jnp.where(j < y, 1.0, 0.0)
    mz[h, 0] = (before[0] - matrix).astype(BF16)
    mz[h, 1] = (before[1] - total).astype(BF16)
    to_heads(mz, m_recv, misc_send.at[4])

    both = jnp.concatenate([bord[...], kvall[...]], axis=2)
    extent = tokens + edge
    both = both.reshape(2 * dim, extent)
    keys, values = both[:dim], both[dim:]
    key_feats = kfbuf[...].reshape(2 * dim, extent)
    token = lax.broadcasted_iota(jnp.int32, (tokens, extent), 0)
    key_at = lax.broadcasted_iota(jnp.int32, (tokens, extent), 1)
    offset = token + edge - key_at
    held = key_at >= lowest
    inside = (offset >= 0) & (offset < WINDOW) & held
    beyond = (offset >= WINDOW) & held
    scores = jnp.dot(queries, keys, preferred_element_type=F32) * (1.0 / math.sqrt(dim))
    far = jnp.dot(query_feats, key_feats, preferred_element_type=F32)
    weights = jnp.where(inside, jnp.exp(scores), 0.0) + jnp.where(beyond, far, 0.0)
    numerator = lax.dot_general(
        weights.astype(BF16), values, contract_last, preferred_element_type=F32
    )
    denominator = jnp.sum(weights, axis=1, keepdims=True)
    o.a_hop(0)
    o.b_far()

    from_heads(mz, m_recv, misc_send.at[4])
    matrix = mz[:, 0].reshape(2 * dim, dim)
    totals = mz[:, 1].reshape(2 * dim, dim)
    numerator = numerator + jnp.dot(query_feats, matrix, preferred_element_type=F32)
    denominator = denominator + jnp.dot(query_feats, totals, preferred_element_type=F32)
    attn[z, core] = (numerator / denominator).astype(BF16)

    a = Spread(
        nz,
        z,
        lambda source: attn.at[source, core],
        lambda place: (c, CORES * place + core),
        misc_send.at[5],
        z_recv,
    )

    def sibling_copy(block, side):
        part = attn.at[block, side]
        return remote(part, part, misc_send.at[6], s_recv.at[block], c, sibling)

    a.start()
    sibling_copy(z, core).start()
    o.a_hop(1)
    for offset in (-1, 1):
        a.wait(offset)
        sibling_copy(a.at(offset), core).start()
    a.wait(-2)
    a.forward_up()
    sibling_copy(a.at(-2), core).start()
    a.wait(2)
    a.forward_down()
    sibling_copy(a.at(2), core).start()
    o.a_hop(2)
    for offset in (-3, 3, -4):
        a.wait(offset)
        sibling_copy(a.at(offset), core).start()
    for offset in range(ny):
        o.b_wait_x(offset)
    o.a_hop(3)
    for offset in range(nz):
        sibling_copy(a.at(offset), 1 - core).wait_recv()

    heads = jnp.concatenate([attn[j // CORES, j % CORES] for j in range(nhead)], axis=1)
    columns = wo_hbm.shape[1]
    tile = 2 * dim

    @pl.loop(0, columns // tile)
    def _(j):
        at = pl.ds(pl.multiple_of(j * tile, tile), tile)
        weights = wfull[:, :, :, at].reshape(nhead * dim, tile)
        out_ref[:, at] = jnp.dot(heads, weights, preferred_element_type=F32).astype(
            BF16
        )

    def sent(ref, sem):
        remote(ref, ref, sem, b_recv, following, h).wait_send()

    q.finish(sent)
    o.finish(sent)
    sent(kvall.at[pl.ds(0, nhead - 1)], misc_send.at[0])
    sent(bord, misc_send.at[1])
    sent(stx.at[pl.ds(0, NX - 1)], misc_send.at[2])
    sent(sty.at[pl.ds(0, ny - 1)], misc_send.at[3])
    sent(mz.at[pl.ds(0, nhead - 1)], misc_send.at[4])
    sent(attn.at[pl.ds(0, nz - 1), 0], misc_send.at[5])
    sent(attn.at[:, 0], misc_send.at[6])
    sent(wkv.at[pl.ds(0, ny - 1)], misc_send.at[8])
    sent(wkv.at[0, pl.ds(0, NX - 1)], misc_send.at[9])


def per_device(activations, w_query, w_keyval, f_query, f_key, w_out):
    nctx, nhead = lax.axis_size("ctx"), lax.axis_size("head")
    ny, nz = nctx // NX, nhead // CORES
    tokens = activations.shape[0]
    rows, width = w_keyval.shape
    half, ohalf = rows // 2, w_out.shape[0] // 2
    dim, columns = f_key.shape[0], w_out.shape[1]
    extent = tokens + 2 * WINDOW
    part = 2 * dim // nhead

    def kernel(*refs):
        sublayer_kernel(nctx, nhead, *refs)

    dma = pltpu.SemaphoreType.DMA
    gather_sems = [
        dma((2,)),
        dma((NX,)),
        dma((2, ny // 2, NX)),
        dma((ny,)),
        dma((ny, NX)),
    ]
    anywhere = pl.BlockSpec(memory_space=pl.ANY)
    vmem = pl.BlockSpec(memory_space=pltpu.VMEM)
    return pl.pallas_call(
        kernel,
        out_shape=jax.ShapeDtypeStruct((tokens, columns), BF16),
        in_specs=[anywhere, anywhere, vmem, vmem, vmem, anywhere],
        out_specs=vmem,
        scratch_shapes=[
            pltpu.VMEM((2 * nctx, tokens, half), BF16),
            pltpu.VMEM((nctx, 2, half, dim), BF16),
            pltpu.VMEM((ny, NX, width, rows), BF16),
            pltpu.VMEM((tokens, dim), F32),
            pltpu.VMEM((nctx, 2, ohalf, columns), BF16),
            pltpu.VMEM((nhead, width, tokens), BF16),
            pltpu.VMEM((nhead, width, 2 * WINDOW), BF16),
            pltpu.VMEM((nhead, part, extent), BF16),
            pltpu.VMEM((NX, 2, part, dim), F32),
            pltpu.VMEM((ny, 2, part, dim), F32),
            pltpu.VMEM((nhead, 2, part, dim), BF16),
            pltpu.VMEM((nz, CORES, tokens, dim), BF16),
            dma,
            dma((4,)),
            *gather_sems,
            *gather_sems,
            dma((NX,)),
            dma((ny,)),
            dma((nhead,)),
            dma,
            dma((NX,)),
            dma((ny,)),
            dma((nhead,)),
            dma((nz,)),
            dma((nz,)),
            dma((10,)),
        ],
        compiler_params=pltpu.CompilerParams(
            collective_id=0, has_side_effects=True, vmem_limit_bytes=56 << 20
        ),
    )(activations, w_query, w_keyval.T, f_query, f_key, w_out)


def solution(mesh):
    in_specs = (
        P("ctx", None),
        P("ctx", "head"),
        P("ctx", "head"),
        P("head", None, None),
        P(),
        P("ctx", "head"),
    )
    out_specs = P("ctx", "head")
    return jax.shard_map(
        per_device, mesh=mesh, in_specs=in_specs, out_specs=out_specs, check_vma=False
    )
```

time: 137 us -> 95.4 us (0.70)
  Pallas kernels: 133 us -> 93.3 us
  local copies, waits for them, and re-layouts: 3.34 us -> 1.87 us
    pallas_call x1, Pallas kernels: 133 us -> 93.3 us  [per_device(): pl.pallas_call(kernel, out_shape=jax.ShapeDtypeStruct((tokens, columns),...]
    unnamed x2 -> x1, local copies, waits for them, and re-layouts: 3.34 us -> 1.87 us
where the time goes in v2:
time: 95.4 us; the launch traced here: 95.2 us
  Pallas kernels  93.3 us (98%)
  local copies, waits for them, and re-layouts  1.87 us (2%)
    pallas_call x1, Pallas kernels, per_device(): pl.pallas_call(kernel, out_shape=jax.ShapeDtypeStruct((tokens, columns),...  93.3 us

profile of v2, /device:TPU:1, one launch (start us, length us, event | category | flops | bytes accessed | tf_op | source)
XLA Modules:
  0.0 95.2 jit_solution(2209936826487501040)
XLA Ops:
  0.0 93.3 %shard_map.64 = bf16[256,1024]{1,0:T(8,128)(2,1)} custom-call(bf16[256,16384]{1,0:T(8,128)(2,1)} %refs_0_.1, bf16[512,128]{1,0:T(8,128)(2,1)} %refs_1_.1, bf16[16,512]{1,0:T(8,128)(2,1)} %bitcast.1, bf16[1,128,128]{2,1,0:T(8,128)(2,1)} %refs_3_.1, bf16[128,128]{1,0:T(8,128)(2,1)} %refs_4_.1, bf16[64,1024]{1,0:T(8,128)(2,1)} %refs_5_.1), custom_call_target="tpu_custom_call" | custom-call | tf_op jit(solution)/shard_map/pallas_call | solution.py:608
  93.3 1.9 %copy.8 = bf16[256,1024]{1,0:T(8,128)(2,1)} copy(bf16[256,1024]{1,0:T(8,128)(2,1)} %shard_map.64) | data formatting | bytes 1048576

commit v3 on v2

--- a/solution.py
+++ b/solution.py
@@ -57,7 +57,7 @@
             part,
             part,
             self.send_sem,
-            self.recv_sem.at[source],
+            self.recv_sem(source),
             *self.device(self.at(offset)),
         )
 
@@ -75,111 +75,148 @@
     def forward_down(self):
         self.copy(self.at(2), -1).start()
 
+    def near(self):
+        self.wait(-2)
+        self.forward_up()
+        self.wait(2)
+        self.forward_down()
+        self.wait(-1)
+        self.wait(1)
+
+    def far(self):
+        for offset in (-3, 3, -4):
+            self.wait(offset)
+
+
+class Ring:
+    def __init__(self, size, place, block, device, send_sem, recv_sem, last):
+        self.size, self.place = size, place
+        self.block, self.device = block, device
+        self.send_sem, self.recv_sem, self.last = send_sem, recv_sem, last
+
+    def at(self, offset):
+        return rem(self.place + offset + self.size, self.size)
+
+    def copy(self, source, way):
+        part = self.block(source)
+        return remote(
+            part,
+            part,
+            self.send_sem,
+            self.recv_sem(source),
+            *self.device(self.at(way)),
+        )
+
+    def ways(self, k):
+        return (1, -1) if k < self.size // 2 - 1 else (self.last,)
+
+    def start(self):
+        for way in self.ways(0):
+            self.copy(self.place, way).start()
+
+    def hop(self, k):
+        onward = self.ways(k + 1) if k + 1 < self.size // 2 else ()
+        for way in self.ways(k):
+            source = self.at(-way * (k + 1))
+            self.copy(source, way).wait_recv()
+            if way in onward:
+                self.copy(source, way).start()
+
 
 class Gather:
-    def __init__(self, buffer, y, x, ny, h, send, ax, ay, by, bx):
-        self.buffer, self.y, self.x, self.ny, self.h = buffer, y, x, ny, h
-        self.send, self.ax, self.ay, self.bx = send, ax, ay, bx
+    def __init__(self, a, b, y, x, ny, h, send, ax, ay, by, bx):
+        self.buf_a, self.buf_b = a, b
+        self.y, self.x, self.ny, self.h = y, x, ny, h
+        self.send, self.ax, self.bx = send, ax, bx
+
+        def device(place):
+            return NX * place + x, h
+
+        def column(j):
+            col = rem(x + j, NX)
+            return Ring(
+                ny,
+                y,
+                lambda source: a.at[NX * source + col],
+                device,
+                send.at[0],
+                lambda source: ay.at[col, source],
+                1 if j < NX // 2 else -1,
+            )
+
+        self.columns = [column(j) for j in range(NX)]
         self.b = Spread(
             ny,
             y,
-            lambda source: buffer.at[NX * source + x, 1],
-            lambda place: (NX * place + x, h),
+            lambda source: b.at[NX * source + x],
+            device,
             send.at[1],
-            by,
-        )
-
-    def ring(self, offset):
+            lambda source: by.at[source],
+        )
+
+    def row(self, offset):
         return rem(self.y + offset + self.ny, self.ny)
 
     def a_copy_x(self, source, to):
-        part = self.buffer.at[NX * self.y + source, 0]
+        part = self.buf_a.at[NX * self.y + source]
         return remote(
             part, part, self.send.at[0], self.ax.at[source], NX * self.y + to, self.h
         )
 
-    def a_start(self):
+    def b_copy_x(self, row, source, to):
+        part = self.buf_b.at[NX * row + source]
+        return remote(
+            part, part, self.send.at[1], self.bx.at[row, source], NX * self.y + to, self.h
+        )
+
+    def start(self):
         for j in range(1, NX):
             self.a_copy_x(self.x, rem(self.x + j, NX)).start()
-
-    def a_wait(self):
-        for j in range(1, NX):
+        self.columns[0].start()
+        self.b.start()
+        self.b_along_x(0)
+
+    def a_row(self):
+        for j in (1, 3, 2):
             self.a_copy_x(rem(self.x + j, NX), self.x).wait_recv()
-
-    def a_sets(self, k):
-        last = k == self.ny // 2 - 1
-        return [
-            (way, col)
-            for col in range(NX)
-            for way in range(2)
-            if not last or (way == 0) == (col < NX // 2)
-        ]
-
-    def a_source(self, way, k):
-        return self.ring(-(k + 1) if way == 0 else k + 1)
-
-    def a_copy(self, way, k, col, row):
-        part = self.buffer.at[NX * row + col, 0]
-        to = self.ring(1 if way == 0 else -1)
-        return remote(
-            part,
-            part,
-            self.send.at[0],
-            self.ay.at[way, k, col],
-            NX * to + self.x,
-            self.h,
-        )
-
-    def a_first(self):
-        for way, col in self.a_sets(0):
-            self.a_copy(way, 0, col, self.y).start()
-
-    def a_hop(self, k):
-        onward = self.a_sets(k + 1) if k + 1 < self.ny // 2 else []
-        for way, col in self.a_sets(k):
-            row = self.a_source(way, k)
-            self.a_copy(way, k, col, row).wait_recv()
-            if (way, col) in onward:
-                self.a_copy(way, k + 1, col, row).start()
-        return [(self.a_source(way, k), col) for way, col in self.a_sets(k)]
-
-    def b_copy_x(self, row, source, to):
-        part = self.buffer.at[NX * row + source, 1]
-        return remote(
-            part, part, self.send.at[1], self.bx.at[row, source], NX * self.y + to, self.h
-        )
+            self.columns[j].start()
 
     def b_along_x(self, offset):
-        row = self.ring(offset)
-        for j in range(1, NX):
-            self.b_copy_x(row, self.x, rem(self.x + j, NX)).start()
+        row = self.row(offset)
+        for way in (1, NX - 1):
+            self.b_copy_x(row, self.x, rem(self.x + way, NX)).start()
+
+    def b_relay(self, *offsets):
+        for offset in offsets:
+            row, way = self.row(offset), 1 if offset % 2 == 0 else NX - 1
+            source = rem(self.x + NX - way, NX)
+            copy = self.b_copy_x(row, source, rem(self.x + way, NX))
+            copy.wait_recv()
+            copy.start()
 
     def b_near(self):
-        for offset in (-1, 1):
-            self.b.wait(offset)
+        self.b.near()
+        for offset in (-1, 1, -2, 2):
             self.b_along_x(offset)
-        self.b.wait(-2)
-        self.b.forward_up()
-        self.b_along_x(-2)
-        self.b.wait(2)
-        self.b.forward_down()
-        self.b_along_x(2)
 
     def b_far(self):
         for offset in (-3, 3, -4):
             self.b.wait(offset)
             self.b_along_x(offset)
 
+    def a_hop(self, k):
+        for j in (1, 3, 2):
+            self.columns[j].hop(k)
+
     def b_wait_x(self, offset):
-        row = self.ring(offset)
-        for j in range(1, NX):
-            self.b_copy_x(row, rem(self.x + j, NX), self.x).wait_recv()
-        return [(row, col) for col in range(NX)]
+        row, way = self.row(offset), 1 if offset % 2 == 0 else NX - 1
+        for source in (rem(self.x + way, NX), rem(self.x + 2, NX)):
+            self.b_copy_x(row, source, self.x).wait_recv()
 
     def finish(self, sent):
         count = NX * self.ny - 1
-        for k in range(2):
-            sent(self.buffer.at[pl.ds(0, count), k], self.send.at[k])
+        sent(self.buf_a.at[pl.ds(0, count)], self.send.at[0])
+        sent(self.buf_b.at[pl.ds(0, count)], self.send.at[1])
 
 
 def sublayer_kernel(
@@ -193,10 +230,13 @@
     wo_hbm,
     out_ref,
     xbuf,
-    wbuf,
-    wkv,
+    wq_a,
+    wq_b,
+    wkv_a,
+    wkv_b,
     acc,
-    wfull,
+    wo_a,
+    wo_b,
     kvall,
     bord,
     kfbuf,
@@ -216,8 +256,10 @@
     o_ay,
     o_by,
     o_bx,
-    w_x,
-    w_y,
+    wa_x,
+    wa_y,
+    wb_y,
+    wb_x,
     kv_recv,
     b_recv,
     x_recv,
@@ -233,8 +275,9 @@
     y, x = div(c, NX), rem(c, NX)
     z, core = div(h, CORES), rem(h, CORES)
     tokens = x_hbm.shape[0]
-    half = wq_hbm.shape[0] // 2
-    ohalf = wo_hbm.shape[0] // 2
+    rows = wq_hbm.shape[0]
+    half = rows // 2
+    low, olow = wq_a.shape[1], wo_a.shape[2]
     dim = fk_ref.shape[0]
     sibling = CORES * z + 1 - core
     following, previous = rem(c + 1, nctx), rem(c + nctx - 1, nctx)
@@ -261,98 +304,111 @@
     greet(previous, h)
 
     own_q = [
+        pltpu.make_async_copy(wq_hbm.at[pl.ds(0, low)], wq_a.at[c], lsem.at[0]),
         pltpu.make_async_copy(
-            wq_hbm.at[pl.ds(half * k, half)], wbuf.at[c, k], lsem.at[k]
-        )
-        for k in range(2)
+            wq_hbm.at[pl.ds(low, rows - low)], wq_b.at[c], lsem.at[1]
+        ),
     ]
     own_o = [
+        pltpu.make_async_copy(wo_hbm.at[:, pl.ds(0, olow)], wo_a.at[c], lsem.at[2]),
         pltpu.make_async_copy(
-            wo_hbm.at[pl.ds(ohalf * k, ohalf)], wfull.at[c, k], lsem.at[2 + k]
-        )
-        for k in range(2)
+            wo_hbm.at[:, pl.ds(olow, wo_hbm.shape[1] - olow)], wo_b.at[c], lsem.at[3]
+        ),
     ]
     for copy in own_q:
         copy.start()
 
-    @pl.loop(0, 2 * nctx)
+    @pl.loop(0, nctx)
     def _(j):
         pltpu.make_async_copy(
-            x_hbm.at[:, pl.ds(pl.multiple_of(j * half, half), half)], xbuf.at[j], xsem
+            x_hbm.at[:, pl.ds(pl.multiple_of(j * rows, rows), rows)], xbuf.at[j], xsem
         ).start()
 
     for copy in own_o:
         copy.start()
-    wkv[y, x] = wkv_ref[...]
+    wkv_a[y, x] = wkv_ref[:, :half]
+    wkv_b[x, y] = wkv_ref[:, half:]
 
     pl.semaphore_wait(barrier, (NX - 1) + (ny - 1) + (nhead - 1) + 2)
 
-    q = Gather(wbuf, y, x, ny, h, q_send, q_ax, q_ay, q_by, q_bx)
-    o = Gather(wfull, y, x, ny, h, o_send, o_ax, o_ay, o_by, o_bx)
-    w = Spread(
-        ny,
-        y,
-        lambda source: wkv.at[source],
-        lambda place: (NX * place + x, h),
-        misc_send.at[8],
-        w_y,
-    )
-
-    def w_copy_x(source, to):
-        part = wkv.at[y, source]
-        return remote(part, part, misc_send.at[9], w_x.at[source], NX * y + to, h)
-
-    for j in range(1, NX):
-        w_copy_x(x, rem(x + j, NX)).start()
+    q = Gather(wq_a, wq_b, y, x, ny, h, q_send, q_ax, q_ay, q_by, q_bx)
+    o = Gather(wo_a, wo_b, y, x, ny, h, o_send, o_ax, o_ay, o_by, o_bx)
+
+    def wa_along_x(source, to):
+        part = wkv_a.at[y, source]
+        return remote(part, part, misc_send.at[8], wa_x.at[source], NX * y + to, h)
+
+    def wa_over_y(source, to):
+        part = wkv_a.at[source]
+        return remote(part, part, misc_send.at[9], wa_y.at[source], NX * to + x, h)
+
+    def wb_over_y(source, to):
+        part = wkv_b.at[x, source]
+        return remote(part, part, misc_send.at[10], wb_y.at[source], NX * to + x, h)
+
+    def wb_along_x(source, to):
+        part = wkv_b.at[source]
+        return remote(part, part, misc_send.at[11], wb_x.at[source], NX * y + to, h)
+
+    def others(place, size, visit):
+        for j in range(1, size):
+            visit(rem(place + j, size))
+
+    others(x, NX, lambda to: wa_along_x(x, to).start())
+    others(y, ny, lambda to: wb_over_y(y, to).start())
+    others(x, NX, lambda source: wa_along_x(source, x).wait_recv())
+    others(y, ny, lambda to: wa_over_y(y, to).start())
+    others(y, ny, lambda source: wb_over_y(source, y).wait_recv())
+    others(x, NX, lambda to: wb_along_x(x, to).start())
     for copy in own_q:
         copy.wait()
-    q.a_start()
-    q.b.start()
-    for j in range(1, NX):
-        w_copy_x(rem(x + j, NX), x).wait_recv()
-    w.start()
-    q.a_wait()
-    q.a_first()
-    q.b_along_x(0)
-
-    def q_product(pairs, k):
+    q.start()
+    pltpu.make_async_copy(xbuf, xbuf, xsem).wait()
+    others(y, ny, lambda source: wa_over_y(source, y).wait_recv())
+    others(x, NX, lambda source: wb_along_x(source, x).wait_recv())
+
+    def a_product(offset):
+        first = NX * q.row(offset)
+        part = jnp.concatenate(
+            [xbuf[first + col, :, :low] for col in range(NX)], axis=1
+        )
+        weights = wq_a[pl.ds(first, NX)].reshape(NX * low, dim)
+        return jnp.dot(part, weights, preferred_element_type=F32)
+
+    def b_product(offset):
+        first = NX * q.row(offset)
         total = None
-        for row, col in pairs:
-            block = NX * row + col
+        for col in range(NX):
             term = jnp.dot(
-                xbuf[2 * block + k], wbuf[block, k], preferred_element_type=F32
+                xbuf[first + col, :, low:],
+                wq_b[first + col],
+                preferred_element_type=F32,
             )
             total = term if total is None else total + term
         return total
 
-    pltpu.make_async_copy(xbuf, xbuf, xsem).wait()
-    acc[...] = q_product([(y, col) for col in range(NX)], 0)
-    q.b_near()
-    for offset in (-1, 1):
-        w.wait(offset)
-    w.wait(-2)
-    w.forward_up()
-    w.wait(2)
-    w.forward_down()
-    pairs0 = q.a_hop(0)
-    for offset in (-3, 3, -4):
-        w.wait(offset)
-
     contract_last = (((1,), (1,)), ((), ()))
 
     def kv_step(block, total):
-        part = wkv[div(block, NX), rem(block, NX)]
-        for k in range(2):
-            total = total + lax.dot_general(
-                part[:, half * k : half * (k + 1)],
-                xbuf[2 * block + k],
+        row, col = div(block, NX), rem(block, NX)
+        return (
+            total
+            + lax.dot_general(
+                wkv_a[row, col],
+                xbuf[block, :, :half],
                 contract_last,
                 preferred_element_type=F32,
             )
-        return total
+            + lax.dot_general(
+                wkv_b[col, row],
+                xbuf[block, :, half:],
+                contract_last,
+                preferred_element_type=F32,
+            )
+        )
 
     own_kv = lax.fori_loop(
-        0, nctx, kv_step, jnp.zeros((wkv.shape[2], tokens), F32), unroll=4
+        0, nctx, kv_step, jnp.zeros((wkv_ref.shape[0], tokens), F32), unroll=4
     )
     kvall[h] = own_kv.astype(BF16)
 
@@ -372,10 +428,10 @@
             ).wait_recv()
 
     to_heads(kvall, kv_recv, misc_send.at[0])
-    q.b_far()
-    pairs1 = q.a_hop(1)
-    acc[...] += q_product(pairs0, 0)
-    acc[...] += q_product(q.b_wait_x(0), 1)
+    q.a_row()
+    q.columns[0].hop(0)
+    q.b_relay(0)
+    q.b_near()
 
     from_heads(kvall, kv_recv, misc_send.at[0])
     border = remote(
@@ -414,10 +470,11 @@
             h,
         ).start()
 
-    pairs2 = q.a_hop(2)
-    acc[...] += q_product(pairs1, 0)
-    for offset in (-1, 1):
-        acc[...] += q_product(q.b_wait_x(offset), 1)
+    q.b_relay(-1, 1, -2, 2)
+    q.columns[0].hop(1)
+    q.b_far()
+    q.a_hop(0)
+    acc[...] = a_product(0)
 
     for j in range(1, NX):
         source = rem(x + j, NX)
@@ -446,23 +503,18 @@
             h,
         ).start()
 
+    q.b_relay(-3, 3, -4)
+    q.columns[0].hop(2)
+    q.a_hop(1)
     for copy in own_o:
         copy.wait()
-    o.a_start()
-    o.b.start()
-    acc[...] += q_product(pairs2, 0)
-    for offset in (-2, 2, -3):
-        acc[...] += q_product(q.b_wait_x(offset), 1)
-    pairs3 = q.a_hop(3)
-    o.a_wait()
-    o.a_first()
-    o.b_along_x(0)
-    for offset in (3, -4):
-        acc[...] += q_product(q.b_wait_x(offset), 1)
-    acc[...] += q_product(pairs3, 0)
-    queries = acc[...].astype(BF16)
-    query_feats = features(jnp.dot(queries, fq_ref[0], preferred_element_type=F32), 1)
-    o.b_near()
+    o.start()
+    for offset in (-1, 1):
+        acc[...] += a_product(offset)
+    for offset in (0, -1, 1):
+        q.b_wait_x(offset)
+        acc[...] += b_product(offset)
+    q.columns[0].hop(3)
 
     border.wait_recv()
     edge_kv = bord[...].reshape(2 * dim, edge)
@@ -490,6 +542,24 @@
     mz[h, 0] = (before[0] - matrix).astype(BF16)
     mz[h, 1] = (before[1] - total).astype(BF16)
     to_heads(mz, m_recv, misc_send.at[4])
+
+    q.a_hop(2)
+    for offset in (-2, 2):
+        acc[...] += a_product(offset)
+        q.b_wait_x(offset)
+        acc[...] += b_product(offset)
+    o.a_row()
+    o.columns[0].hop(0)
+    o.b_relay(0)
+    o.b_near()
+    for offset in (-3, 3, -4):
+        q.b_wait_x(offset)
+        acc[...] += b_product(offset)
+    q.a_hop(3)
+    for offset in (-3, 3, -4):
+        acc[...] += a_product(offset)
+    queries = acc[...].astype(BF16)
+    query_feats = features(jnp.dot(queries, fq_ref[0], preferred_element_type=F32), 1)
 
     both = jnp.concatenate([bord[...], kvall[...]], axis=2)
     extent = tokens + edge
@@ -509,8 +579,6 @@
         weights.astype(BF16), values, contract_last, preferred_element_type=F32
     )
     denominator = jnp.sum(weights, axis=1, keepdims=True)
-    o.a_hop(0)
-    o.b_far()
 
     from_heads(mz, m_recv, misc_send.at[4])
     matrix = mz[:, 0].reshape(2 * dim, dim)
@@ -525,7 +593,7 @@
         lambda source: attn.at[source, core],
         lambda place: (c, CORES * place + core),
         misc_send.at[5],
-        z_recv,
+        lambda source: z_recv.at[source],
     )
 
     def sibling_copy(block, side):
@@ -534,20 +602,24 @@
 
     a.start()
     sibling_copy(z, core).start()
-    o.a_hop(1)
-    for offset in (-1, 1):
-        a.wait(offset)
-        sibling_copy(a.at(offset), core).start()
+    o.a_hop(0)
+    o.columns[0].hop(1)
+    o.b_relay(-1, 1, -2, 2)
+    o.b_far()
     a.wait(-2)
     a.forward_up()
     sibling_copy(a.at(-2), core).start()
     a.wait(2)
     a.forward_down()
     sibling_copy(a.at(2), core).start()
-    o.a_hop(2)
-    for offset in (-3, 3, -4):
+    o.a_hop(1)
+    o.columns[0].hop(2)
+    o.b_relay(-3, 3, -4)
+    for offset in (-1, 1, -3, 3, -4):
         a.wait(offset)
         sibling_copy(a.at(offset), core).start()
+    o.a_hop(2)
+    o.columns[0].hop(3)
     for offset in range(ny):
         o.b_wait_x(offset)
     o.a_hop(3)
@@ -555,16 +627,15 @@
         sibling_copy(a.at(offset), 1 - core).wait_recv()
 
     heads = jnp.concatenate([attn[j // CORES, j % CORES] for j in range(nhead)], axis=1)
-    columns = wo_hbm.shape[1]
-    tile = 2 * dim
-
-    @pl.loop(0, columns // tile)
-    def _(j):
-        at = pl.ds(pl.multiple_of(j * tile, tile), tile)
-        weights = wfull[:, :, :, at].reshape(nhead * dim, tile)
-        out_ref[:, at] = jnp.dot(heads, weights, preferred_element_type=F32).astype(
-            BF16
-        )
+    start = 0
+    for weights in (wo_a, wo_b):
+        for at in range(0, weights.shape[2], 2 * dim):
+            size = min(2 * dim, weights.shape[2] - at)
+            tile = weights[:, :, at : at + size].reshape(nhead * dim, size)
+            out_ref[:, start : start + size] = jnp.dot(
+                heads, tile, preferred_element_type=F32
+            ).astype(BF16)
+            start += size
 
     def sent(ref, sem):
         remote(ref, ref, sem, b_recv, following, h).wait_send()
@@ -578,8 +649,10 @@
     sent(mz.at[pl.ds(0, nhead - 1)], misc_send.at[4])
     sent(attn.at[pl.ds(0, nz - 1), 0], misc_send.at[5])
     sent(attn.at[:, 0], misc_send.at[6])
-    sent(wkv.at[pl.ds(0, ny - 1)], misc_send.at[8])
-    sent(wkv.at[0, pl.ds(0, NX - 1)], misc_send.at[9])
+    sent(wkv_a.at[0, pl.ds(0, NX - 1)], misc_send.at[8])
+    sent(wkv_a.at[pl.ds(0, ny - 1)], misc_send.at[9])
+    sent(wkv_b.at[0, pl.ds(0, ny - 1)], misc_send.at[10])
+    sent(wkv_b.at[pl.ds(0, NX - 1)], misc_send.at[11])
 
 
 def per_device(activations, w_query, w_keyval, f_query, f_key, w_out):
@@ -587,8 +660,9 @@
     ny, nz = nctx // NX, nhead // CORES
     tokens = activations.shape[0]
     rows, width = w_keyval.shape
-    half, ohalf = rows // 2, w_out.shape[0] // 2
+    low, orows = rows // 2, w_out.shape[0]
     dim, columns = f_key.shape[0], w_out.shape[1]
+    olow = columns // 2
     extent = tokens + 2 * WINDOW
     part = 2 * dim // nhead
 
@@ -599,7 +673,7 @@
     gather_sems = [
         dma((2,)),
         dma((NX,)),
-        dma((2, ny // 2, NX)),
+        dma((NX, ny)),
         dma((ny,)),
         dma((ny, NX)),
     ]
@@ -611,11 +685,14 @@
         in_specs=[anywhere, anywhere, vmem, vmem, vmem, anywhere],
         out_specs=vmem,
         scratch_shapes=[
-            pltpu.VMEM((2 * nctx, tokens, half), BF16),
-            pltpu.VMEM((nctx, 2, half, dim), BF16),
-            pltpu.VMEM((ny, NX, width, rows), BF16),
+            pltpu.VMEM((nctx, tokens, rows), BF16),
+            pltpu.VMEM((nctx, low, dim), BF16),
+            pltpu.VMEM((nctx, rows - low, dim), BF16),
+            pltpu.VMEM((ny, NX, width, rows // 2), BF16),
+            pltpu.VMEM((NX, ny, width, rows // 2), BF16),
             pltpu.VMEM((tokens, dim), F32),
-            pltpu.VMEM((nctx, 2, ohalf, columns), BF16),
+            pltpu.VMEM((nctx, orows, olow), BF16),
+            pltpu.VMEM((nctx, orows, columns - olow), BF16),
             pltpu.VMEM((nhead, width, tokens), BF16),
             pltpu.VMEM((nhead, width, 2 * WINDOW), BF16),
             pltpu.VMEM((nhead, part, extent), BF16),
@@ -629,6 +706,8 @@
             *gather_sems,
             dma((NX,)),
             dma((ny,)),
+            dma((ny,)),
+            dma((NX,)),
             dma((nhead,)),
             dma,
             dma((NX,)),
@@ -636,7 +715,7 @@
             dma((nhead,)),
             dma((nz,)),
             dma((nz,)),
-            dma((10,)),
+            dma((12,)),
         ],
         compiler_params=pltpu.CompilerParams(
             collective_id=0, has_side_effects=True, vmem_limit_bytes=56 << 20

time: 95.4 us -> 92 us (0.964)
  Pallas kernels: 93.3 us -> 89.8 us
    pallas_call x1, Pallas kernels: 93.3 us -> 89.8 us  [per_device(): pl.pallas_call(kernel, out_shape=jax.ShapeDtypeStruct((tokens, columns),...]
where the time goes in v3:
time: 92 us; the launch traced here: 91.6 us
  Pallas kernels  89.8 us (98%)
  local copies, waits for them, and re-layouts  1.87 us (2%)
    pallas_call x1, Pallas kernels, per_device(): pl.pallas_call(kernel, out_shape=jax.ShapeDtypeStruct((tokens, columns),...  89.8 us
    unnamed x1, local copies, waits for them, and re-layouts  1.87 us

profile of v3, /device:TPU:1, one launch (start us, length us, event | category | flops | bytes accessed | tf_op | source)
XLA Modules:
  0.0 91.6 jit_solution(10930889978439680277)
XLA Ops:
  0.0 89.8 %shard_map.64 = bf16[256,1024]{1,0:T(8,128)(2,1)} custom-call(bf16[256,16384]{1,0:T(8,128)(2,1)} %refs_0_.1, bf16[512,128]{1,0:T(8,128)(2,1)} %refs_1_.1, bf16[16,512]{1,0:T(8,128)(2,1)} %bitcast.1, bf16[1,128,128]{2,1,0:T(8,128)(2,1)} %refs_3_.1, bf16[128,128]{1,0:T(8,128)(2,1)} %refs_4_.1, bf16[64,1024]{1,0:T(8,128)(2,1)} %refs_5_.1), custom_call_target="tpu_custom_call" | custom-call | tf_op jit(solution)/shard_map/pallas_call | solution.py:682
  89.8 1.9 %copy.8 = bf16[256,1024]{1,0:T(8,128)(2,1)} copy(bf16[256,1024]{1,0:T(8,128)(2,1)} %shard_map.64) | data formatting | bytes 1048576

commit v4 on v3

--- a/solution.py
+++ b/solution.py
@@ -662,7 +662,7 @@
     rows, width = w_keyval.shape
     low, orows = rows // 2, w_out.shape[0]
     dim, columns = f_key.shape[0], w_out.shape[1]
-    olow = columns // 2
+    olow = 3 * columns // 8
     extent = tokens + 2 * WINDOW
     part = 2 * dim // nhead
 

time: 92 us -> 90 us (0.978)
  Pallas kernels: 89.8 us -> 87.5 us
    pallas_call x1, Pallas kernels: 89.8 us -> 87.5 us  [per_device(): pl.pallas_call(kernel, out_shape=jax.ShapeDtypeStruct((tokens, columns),...]
where the time goes in v4:
time: 90 us; the launch traced here: 89.4 us
  Pallas kernels  87.5 us (97%)
  local copies, waits for them, and re-layouts  1.87 us (2%)
    pallas_call x1, Pallas kernels, per_device(): pl.pallas_call(kernel, out_shape=jax.ShapeDtypeStruct((tokens, columns),...  87.5 us
    unnamed x1, local copies, waits for them, and re-layouts  1.87 us

profile of v4, /device:TPU:1, one launch (start us, length us, event | category | flops | bytes accessed | tf_op | source)
XLA Modules:
  0.0 89.4 jit_solution(3887862650629849422)
XLA Ops:
  0.0 87.5 %shard_map.64 = bf16[256,1024]{1,0:T(8,128)(2,1)} custom-call(bf16[256,16384]{1,0:T(8,128)(2,1)} %refs_0_.1, bf16[512,128]{1,0:T(8,128)(2,1)} %refs_1_.1, bf16[16,512]{1,0:T(8,128)(2,1)} %bitcast.1, bf16[1,128,128]{2,1,0:T(8,128)(2,1)} %refs_3_.1, bf16[128,128]{1,0:T(8,128)(2,1)} %refs_4_.1, bf16[64,1024]{1,0:T(8,128)(2,1)} %refs_5_.1), custom_call_target="tpu_custom_call" | custom-call | tf_op jit(solution)/shard_map/pallas_call | solution.py:682
  87.5 1.9 %copy.8 = bf16[256,1024]{1,0:T(8,128)(2,1)} copy(bf16[256,1024]{1,0:T(8,128)(2,1)} %shard_map.64) | data formatting | bytes 1048576

commit v5 on v4

--- a/solution.py
+++ b/solution.py
@@ -622,13 +622,13 @@
     o.columns[0].hop(3)
     for offset in range(ny):
         o.b_wait_x(offset)
-    o.a_hop(3)
     for offset in range(nz):
         sibling_copy(a.at(offset), 1 - core).wait_recv()
 
     heads = jnp.concatenate([attn[j // CORES, j % CORES] for j in range(nhead)], axis=1)
-    start = 0
-    for weights in (wo_a, wo_b):
+    for weights, start in ((wo_b, olow), (wo_a, 0)):
+        if start == 0:
+            o.a_hop(3)
         for at in range(0, weights.shape[2], 2 * dim):
             size = min(2 * dim, weights.shape[2] - at)
             tile = weights[:, :, at : at + size].reshape(nhead * dim, size)

time: 90 us -> 89.9 us (level)
  no operation moved by 1% of the time
where the time goes in v5:
time: 89.9 us; the launch traced here: 89.2 us
  Pallas kernels  87.3 us (97%)
  local copies, waits for them, and re-layouts  1.87 us (2%)
    pallas_call x1, Pallas kernels, per_device(): pl.pallas_call(kernel, out_shape=jax.ShapeDtypeStruct((tokens, columns),...  87.3 us
    unnamed x1, local copies, waits for them, and re-layouts  1.87 us

profile of v5, /device:TPU:1, one launch (start us, length us, event | category | flops | bytes accessed | tf_op | source)
XLA Modules:
  0.0 89.2 jit_solution(7329948107036848681)
XLA Ops:
  0.0 87.3 %shard_map.64 = bf16[256,1024]{1,0:T(8,128)(2,1)} custom-call(bf16[256,16384]{1,0:T(8,128)(2,1)} %refs_0_.1, bf16[512,128]{1,0:T(8,128)(2,1)} %refs_1_.1, bf16[16,512]{1,0:T(8,128)(2,1)} %bitcast.1, bf16[1,128,128]{2,1,0:T(8,128)(2,1)} %refs_3_.1, bf16[128,128]{1,0:T(8,128)(2,1)} %refs_4_.1, bf16[64,1024]{1,0:T(8,128)(2,1)} %refs_5_.1), custom_call_target="tpu_custom_call" | custom-call | tf_op jit(solution)/shard_map/pallas_call | solution.py:682
  87.3 1.9 %copy.8 = bf16[256,1024]{1,0:T(8,128)(2,1)} copy(bf16[256,1024]{1,0:T(8,128)(2,1)} %shard_map.64) | data formatting | bytes 1048576
